TPU v7x, 128 devices: a whole 4x4x4 slice. The times are simulated.
128 devices in a mesh: seq: 32 (over y, z, core), head: 4 (over x).
Axes of the slice: x: 4, y: 4, z: 4, core: 2. Of those that a mesh axis runs over, the one named last changes fastest.
Arguments:
- vision: bfloat16 [65536, 7680], P(('seq', 'head')), may hold values from -6 to 6
- w_key: bfloat16 [7680, 512], replicated, may hold values from -0.0625 to 0.0625
- w_value: bfloat16 [7680, 512], replicated, may hold values from -0.0625 to 0.0625
- queries: bfloat16 [256, 4096], P('seq', 'head'), may hold values from -240 to 240
- w_out: bfloat16 [4096, 8192], P('head', 'seq'), may hold values from -0.09375 to 0.09375
Outputs:
- mixed: bfloat16 [256, 8192], P('head', 'seq')
All inputs are finite; a program needn't handle non-finite values.
Results may differ from a plain program's by a relative error of at most 0.03.
Values may be sent and summed in bfloat16 or wider, within the bound.
No kernel may reach another device: no remote copies, remote signals or barrier semaphores. Data moves between devices by JAX's collectives and lax.ppermute only.
A program may use at most 128 MiB of HBM per device.

v0:
```python
import jax
import jax.numpy as jnp
from jax import lax
from jax.sharding import PartitionSpec as P

HD = 128


def scale_rows(partial_value, factor):
    return (
        partial_value.reshape(factor.shape[0], factor.shape[1], -1) * factor[:, :, None]
    ).reshape(factor.shape[0], -1)


def divide_rows(partial_value, denom):
    return (partial_value.reshape(denom.shape[0], denom.shape[1], -1) / denom[:, :, None]).reshape(
        denom.shape[0], -1
    )


def attend(queries_all, keys_here, values_here):
    head_size = HD
    kv_local = keys_here.shape[1] // head_size
    text_rows = queries_all.shape[0]
    q_heads = queries_all.shape[1] // head_size
    group_size = q_heads // kv_local
    grouped = queries_all.reshape(text_rows, kv_local, group_size, head_size)
    key_heads = keys_here.reshape(keys_here.shape[0], kv_local, head_size)
    value_heads = values_here.reshape(values_here.shape[0], kv_local, head_size)
    scores = jnp.einsum(
        "tkgd,nkd->kgtn", grouped, key_heads, preferred_element_type=jnp.float32
    ) * head_size ** (-0.5)
    maxima = jnp.max(scores, axis=-1)
    powers = jnp.exp(scores - maxima[..., None])
    totals = jnp.sum(powers, axis=-1)
    partial_value = jnp.einsum(
        "kgtn,nkd->tkgd",
        powers.astype(jnp.bfloat16),
        value_heads,
        preferred_element_type=jnp.float32,
    )
    partial_value = partial_value.reshape(text_rows, q_heads * head_size)
    maxima = maxima.transpose(2, 0, 1).reshape(text_rows, q_heads)
    totals = totals.transpose(2, 0, 1).reshape(text_rows, q_heads)
    return (maxima, totals, partial_value)


def shards(vision, w_key, w_value, queries, w_out):
    keys = jnp.dot(vision, w_key, preferred_element_type=jnp.float32).astype(jnp.bfloat16)
    values = jnp.dot(vision, w_value, preferred_element_type=jnp.float32).astype(jnp.bfloat16)
    keys_here, values_here = (
        lax.all_to_all(keys, "head", split_axis=1, concat_axis=0, tiled=True),
        lax.all_to_all(values, "head", split_axis=1, concat_axis=0, tiled=True),
    )
    queries_all = lax.all_gather(queries, "seq", axis=0, tiled=True)
    maxima, totals, partial_value = attend(queries_all, keys_here, values_here)
    global_max = lax.pmax(maxima, "seq")
    factor = jnp.exp(maxima - global_max)
    denom, numer = (
        lax.psum((totals * factor).astype(jnp.bfloat16), "seq").astype(jnp.float32),
        lax.psum(scale_rows(partial_value, factor).astype(jnp.bfloat16), "seq").astype(jnp.float32),
    )
    attended = divide_rows(numer, denom).astype(jnp.bfloat16)
    return lax.psum_scatter(
        jnp.dot(attended, w_out, preferred_element_type=jnp.float32).astype(jnp.bfloat16),
        "head",
        scatter_dimension=0,
        tiled=True,
    )


def solution(mesh):
    placed = (P(("seq", "head"), None), P(), P(), P("seq", "head"), P("head", "seq"))
    return jax.shard_map(
        shards, mesh=mesh, in_specs=placed, out_specs=P("head", "seq"), check_vma=False
    )
```

profile of v0, /device:TPU:0, one launch (start us, length us, event | category | flops | bytes accessed | tf_op | source)
XLA Modules:
  0.0 286.8 jit_solution(6718358822578115209)
XLA Ops:
  6.5 0.0 copy-start
  6.5 10.6 %convolution_convert_fusion.1 = bf16[512,512]{0,1:T(8,128)(2,1)} fusion(bf16[512,7680]{1,0:T(8,128)(2,1)} %param.5, bf16[7680,512]{1,0:T(8,128)(2,1)} %param.7), kind=kOutput, calls=%fused_computation.8 | convolution fusion | flops 4026793984 | bytes 16252928 | tf_op jit(solution)/shard_map/dot_general | solution.py:50
  17.1 0.0 copy-start.1
  17.1 4.5 %all-to-all-start = ((bf16[512,4,128]{0,2,1:T(8,128)(2,1)}), bf16[512,4,128]{0,2,1:T(8,128)(2,1)S(1)}, u32[]{:S(2)}, u32[]{:S(2)}) async-start(bf16[512,4,128]{0,2,1:T(8,128)(2,1)} %bitcast), calls=%async_computation | async-start | bytes 1048576 | tf_op jit(solution)/shard_map/all_to_all | solution.py:53
  21.7 10.5 %convolution_convert_fusion = bf16[512,512]{0,1:T(8,128)(2,1)} fusion(bf16[512,7680]{1,0:T(8,128)(2,1)} %param.5, bf16[7680,512]{1,0:T(8,128)(2,1)} %param.6), kind=kOutput, calls=%fused_computation.7 | convolution fusion | flops 4026793984 | bytes 16252928 | tf_op jit(solution)/shard_map/dot_general | solution.py:49
  32.2 0.0 all-to-all-done
  32.2 4.8 %all-to-all-start.1 = ((bf16[512,4,128]{0,2,1:T(8,128)(2,1)}), bf16[512,4,128]{0,2,1:T(8,128)(2,1)S(1)}, u32[]{:S(2)}, u32[]{:S(2)}) async-start(bf16[512,4,128]{0,2,1:T(8,128)(2,1)} %bitcast.2), calls=%async_computation.1 | async-start | bytes 1048576 | tf_op jit(solution)/shard_map/all_to_all | solution.py:52
  37.0 0.0 all-reduce.2.cloned.1.call-start
  37.0 0.0 copy-done.1
  37.0 26.5 %all_gather.3 = bf16[256,1024]{1,0:T(8,128)(2,1)S(1)} all-gather(bf16[8,1024]{1,0:T(8,128)(2,1)S(1)} %copy-done.1), channel_id=1, replica_groups=mesh['seq'=32,'head'=4] {'seq'}, dimensions={0}, use_global_device_ids=true | all-gather | bytes 540672 | tf_op jit(solution)/shard_map/all_gather | solution.py:55
  63.5 0.2 copy.16
  63.7 0.4 copy.14
  64.1 0.4 reshape.57
  64.5 0.0 all-to-all-done.1
  64.5 0.3 copy.15
  64.8 8.0 %bitcast_reduce_fusion = (f32[8,256]{1,0:T(8,128)S(1)}, f32[2048,256,8]{1,0,2:T(8,128)}) fusion(bf16[2048,128,1]{1,0,2:T(8,128)(2,1)S(1)} %bitcast.66, bf16[256,8,128]{0,2,1:T(8,128)(2,1)S(1)} %bitcast.65), kind=kOutput, calls=%fused_computation.1 | convolution fusion | flops 1082128384 | bytes 17833984 | tf_op jit(solution)/shard_map/tkgd,nkd->kgtn/dot_general | solution.py:30
  72.8 8.5 %fusion.1 = f32[8,256]{1,0:T(8,128)S(1)} fusion(f32[2048,256,8]{1,0,2:T(8,128)} %get-tuple-element.8, f32[8,256]{1,0:T(8,128)S(1)} %get-tuple-element.7), kind=kLoop, calls=%fused_computation.3 | loop fusion | flops 12580864 | bytes 16793600 | tf_op jit(solution)/shard_map/reduce_sum | solution.py:35
  81.3 7.4 %fusion.4 = f32[128,8,256]{2,0,1:T(8,128)S(1)} fusion(bf16[2048,128,1]{0,1,2:T(8,128)(2,1)S(1)} %reshape.57, f32[2048,256,8]{1,0,2:T(8,128)} %get-tuple-element.8, f32[8,256]{1,0:T(8,128)S(1)} %get-tuple-element.7), kind=kOutput, calls=%fused_computation.6 | convolution fusion | flops 1086324736 | bytes 18358272 | tf_op jit(solution)/shard_map/kgtn,nkd->tkgd/dot_general | solution.py:36
  88.7 66.3 %pmax.7 = f32[256,8]{0,1:T(8,128)S(1)} all-reduce(f32[256,8]{0,1:T(8,128)S(1)} %bitcast.69), channel_id=1, replica_groups=mesh['seq'=32,'head'=4] {'seq'}, use_global_device_ids=true, to_apply=%region_1.0 | all-reduce | flops 2048 | bytes 16384 | tf_op jit(solution)/shard_map/pmax | solution.py:57
  155.1 0.9 fusion.6
  156.0 0.0 all-reduce.2.cloned.1.call-update
  156.0 0.0 reduce-scatter.2.cloned.1.call-start
  156.0 62.8 %psum.15 = bf16[256,8]{0,1:T(8,128)(2,1)S(1)} all-reduce(bf16[256,8]{0,1:T(8,128)(2,1)S(1)} %get-tuple-element.5), channel_id=1, replica_groups=mesh['seq'=32,'head'=4] {'seq'}, use_global_device_ids=true, to_apply=%region_4.0 | all-reduce | flops 2048 | bytes 8192 | tf_op jit(solution)/shard_map/psum | solution.py:60
  218.8 38.6 %all-reduce.2.cloned.1.call-done = bf16[256,1024]{0,1:T(8,128)(2,1)} async-done(((bf16[256,1024]{0,1:T(8,128)(2,1)}), bf16[256,1024]{0,1:T(8,128)(2,1)}) %all-reduce.2.cloned.1.call-update) | async-done | bytes 524304 | tf_op jit(solution)/shard_map/psum | solution.py:61
  257.4 1.1 fusion.7
  258.6 0.0 copy-done
  258.6 1.0 convolution_convert_fusion.2
  259.6 0.0 reduce-scatter.2.cloned.1.call-update
  259.6 20.4 %reduce-scatter.2.cloned.1.call-done = bf16[64,256]{1,0:T(8,128)(2,1)} async-done(((bf16[256,256]{1,0:T(8,128)(2,1)}), bf16[64,256]{1,0:T(8,128)(2,1)}) %reduce-scatter.2.cloned.1.call-update) | async-done | bytes 32784 | tf_op jit(solution)/shard_map/reduce_scatter | solution.py:64
  (2 shorter events, 0.0 us)
Async XLA Ops:
  6.5 252.0 %copy-start = (bf16[1024,256]{1,0:T(8,128)(2,1)S(1)}, bf16[1024,256]{1,0:T(8,128)(2,1)}, u32[]{:S(2)}) copy-start(bf16[1024,256]{1,0:T(8,128)(2,1)} %param.9) | copy-start | bytes 1572868
  17.1 19.9 %copy-start.1 = (bf16[8,1024]{1,0:T(8,128)(2,1)S(1)}, bf16[8,1024]{1,0:T(8,128)(2,1)}, u32[]{:S(2)}) copy-start(bf16[8,1024]{1,0:T(8,128)(2,1)} %param.8) | copy-start | bytes 49156
  17.1 15.1 %all-to-all-start = ((bf16[512,4,128]{0,2,1:T(8,128)(2,1)}), bf16[512,4,128]{0,2,1:T(8,128)(2,1)S(1)}, u32[]{:S(2)}, u32[]{:S(2)}) async-start(bf16[512,4,128]{0,2,1:T(8,128)(2,1)} %bitcast), calls=%async_computation | async-start | bytes 1048576 | tf_op jit(solution)/shard_map/all_to_all | solution.py:53
  32.2 32.3 %all-to-all-start.1 = ((bf16[512,4,128]{0,2,1:T(8,128)(2,1)}), bf16[512,4,128]{0,2,1:T(8,128)(2,1)S(1)}, u32[]{:S(2)}, u32[]{:S(2)}) async-start(bf16[512,4,128]{0,2,1:T(8,128)(2,1)} %bitcast.2), calls=%async_computation.1 | async-start | bytes 1048576 | tf_op jit(solution)/shard_map/all_to_all | solution.py:52
  37.0 220.4 %all-reduce.2.cloned.1.call-start = ((), (), s32[]{:S(2)}) async-start(), calls=%async_computation.3 | async-start | bytes 1048576 | tf_op jit(solution)/shard_map/psum | solution.py:61
  156.0 124.0 %reduce-scatter.2.cloned.1.call-start = ((), (), s32[]{:S(2)}) async-start(), calls=%async_computation.4 | async-start | bytes 163840 | tf_op jit(solution)/shard_map/reduce_scatter | solution.py:64
Sparse Core Ops, SparseCore 0:
  156.1 101.2 all-reduce.1
  259.8 20.1 reduce-scatter.1
where the time goes:
time: 287 us
  blocking collectives  156 us (54%)
  waiting for transfers between devices  59 us (21%)
  matrix products  37.6 us (13%)
  between operations  13.5 us (5%)
  other arithmetic  10.5 us (4%)
  starting transfers between devices  9.38 us (3%)
    pmax x1, blocking collectives, shards(): global_max = lax.pmax(maxima, 'seq')  66.3 us
    psum x1, blocking collectives, shards(): lax.psum((totals * factor).astype(jnp.bfloat16), 'seq').astype(jnp.float32)  62.8 us
    psum x1, waiting for transfers between devices, shards(): lax.psum(scale_rows(partial_value, factor).astype(jnp.bfloat16), 'seq')  38.6 us
    all_gather x1, blocking collectives, shards(): queries_all = lax.all_gather(queries, 'seq', axis=0, tiled=True)  26.5 us
    reduce_scatter x1, waiting for transfers between devices, shards(): lax.psum_scatter(jnp.dot(attended, w_out, preferred_element_type=jnp.floa...  20.4 us
    dot_general x1, matrix products, shards(): jnp.dot(vision, w_value, preferred_element_type=jnp.float32)  10.6 us
    dot_general x1, matrix products, shards(): jnp.dot(vision, w_key, preferred_element_type=jnp.float32)  10.5 us
    reduce_sum x1, other arithmetic, attend(): totals = jnp.sum(powers, axis=-1)  8.48 us
  transfers between devices with their start and end apart: 4, of which 2 were waited for; matrix products, arithmetic and copies ran while one was open for 4% of the time, Pallas kernels for 0%

commit v1 on v0

--- a/solution.py
+++ b/solution.py
@@ -58,7 +58,9 @@
     factor = jnp.exp(maxima - global_max)
     denom, numer = (
         lax.psum((totals * factor).astype(jnp.bfloat16), "seq").astype(jnp.float32),
-        lax.psum(scale_rows(partial_value, factor).astype(jnp.bfloat16), "seq").astype(jnp.float32),
+        jnp.sum(
+            lax.all_gather(scale_rows(partial_value, factor).astype(jnp.bfloat16), "seq"), axis=0
+        ).astype(jnp.float32),
     )
     attended = divide_rows(numer, denom).astype(jnp.bfloat16)
     return lax.psum_scatter(

time: 287 us -> 267 us (0.930)
  waiting for transfers between devices: 59 us -> 25.1 us
  other arithmetic: 10.5 us -> 18.6 us
  local copies, waits for them, and re-layouts: 1.27 us -> 4.65 us
    psum x1 -> x0, waiting for transfers between devices: 38.6 us -> none  [shards(): lax.psum(scale_rows(partial_value, factor).astype(jnp.bfloat16), 'seq')]
    reduce_sum x0 -> x1, other arithmetic: none -> 9.07 us  [shards(): jnp.sum(lax.all_gather(scale_rows(partial_value, factor).astype(jnp.bfloa...]
    all_gather x0 -> x1, waiting for transfers between devices: none -> 5.12 us  [shards(): lax.all_gather(scale_rows(partial_value, factor).astype(jnp.bfloat16), 's...]
where the time goes in v1:
time: 267 us; the launch traced here: 266 us
  blocking collectives  158 us (59%)
  matrix products  37.5 us (14%)
  waiting for transfers between devices  25.1 us (9%)
  other arithmetic  18.6 us (7%)
  between operations  13.5 us (5%)
  starting transfers between devices  9.38 us (4%)
  local copies, waits for them, and re-layouts  4.65 us (2%)
    pmax x1, blocking collectives, shards(): global_max = lax.pmax(maxima, 'seq')  66.3 us
    psum x1, blocking collectives, shards(): lax.psum((totals * factor).astype(jnp.bfloat16), 'seq').astype(jnp.float32)  64.8 us
    all_gather x1, blocking collectives, shards(): queries_all = lax.all_gather(queries, 'seq', axis=0, tiled=True)  26.5 us
    reduce_scatter x1, waiting for transfers between devices, shards(): lax.psum_scatter(jnp.dot(attended, w_out, preferred_element_type=jnp.floa...  19.9 us
    dot_general x1, matrix products, shards(): jnp.dot(vision, w_key, preferred_element_type=jnp.float32)  10.6 us
    dot_general x1, matrix products, shards(): jnp.dot(vision, w_value, preferred_element_type=jnp.float32)  10.5 us
    reduce_sum x1, other arithmetic, shards(): jnp.sum(lax.all_gather(scale_rows(partial_value, factor).astype(jnp.bfloa...  9.07 us
    reduce_sum x1, other arithmetic, attend(): totals = jnp.sum(powers, axis=-1)  8.49 us
  transfers between devices with their start and end apart: 4, of which 2 were waited for; matrix products, arithmetic and copies ran while one was open for 4% of the time, Pallas kernels for 0%

profile of v1, /device:TPU:0, one launch (start us, length us, event | category | flops | bytes accessed | tf_op | source)
XLA Modules:
  0.0 266.3 jit_solution(15861211125281841099)
XLA Ops:
  6.5 0.0 copy-start
  6.5 10.6 %convolution_convert_fusion = bf16[512,512]{0,1:T(8,128)(2,1)} fusion(bf16[512,7680]{1,0:T(8,128)(2,1)} %param.5, bf16[7680,512]{1,0:T(8,128)(2,1)} %param.6), kind=kOutput, calls=%fused_computation.7 | convolution fusion | flops 4026793984 | bytes 16252928 | tf_op jit(solution)/shard_map/dot_general | solution.py:49
  17.1 4.5 %all-to-all-start.1 = ((bf16[512,4,128]{0,2,1:T(8,128)(2,1)}), bf16[512,4,128]{0,2,1:T(8,128)(2,1)S(1)}, u32[]{:S(2)}, u32[]{:S(2)}) async-start(bf16[512,4,128]{0,2,1:T(8,128)(2,1)} %bitcast.2), calls=%async_computation.1 | async-start | bytes 1048576 | tf_op jit(solution)/shard_map/all_to_all | solution.py:52
  21.7 10.5 %convolution_convert_fusion.1 = bf16[512,512]{0,1:T(8,128)(2,1)} fusion(bf16[512,7680]{1,0:T(8,128)(2,1)} %param.5, bf16[7680,512]{1,0:T(8,128)(2,1)} %param.7), kind=kOutput, calls=%fused_computation.8 | convolution fusion | flops 4026793984 | bytes 16252928 | tf_op jit(solution)/shard_map/dot_general | solution.py:50
  32.2 0.0 all-to-all-done.1
  32.2 4.8 %all-to-all-start = ((bf16[512,4,128]{0,2,1:T(8,128)(2,1)}), bf16[512,4,128]{0,2,1:T(8,128)(2,1)S(1)}, u32[]{:S(2)}, u32[]{:S(2)}) async-start(bf16[512,4,128]{0,2,1:T(8,128)(2,1)} %bitcast), calls=%async_computation | async-start | bytes 1048576 | tf_op jit(solution)/shard_map/all_to_all | solution.py:53
  37.0 0.0 copy-done.1
  37.0 26.5 %all_gather.7 = bf16[256,1024]{1,0:T(8,128)(2,1)S(1)} all-gather(bf16[8,1024]{1,0:T(8,128)(2,1)S(1)} %copy-done.1), channel_id=1, replica_groups=mesh['seq'=32,'head'=4] {'seq'}, dimensions={0}, use_global_device_ids=true | all-gather | bytes 540672 | tf_op jit(solution)/shard_map/all_gather | solution.py:55
  63.5 0.2 copy.18
  63.7 0.3 copy.17
  64.0 0.0 all-to-all-done
  64.0 0.4 copy.16
  64.4 0.4 reshape.78
  64.8 8.0 %bitcast_reduce_fusion = (f32[8,256]{1,0:T(8,128)S(1)}, f32[2048,256,8]{1,0,2:T(8,128)}) fusion(bf16[2048,128,1]{1,0,2:T(8,128)(2,1)S(1)} %bitcast.62, bf16[256,8,128]{0,2,1:T(8,128)(2,1)S(1)} %bitcast.61), kind=kOutput, calls=%fused_computation.1 | convolution fusion | flops 1082128384 | bytes 17833984 | tf_op jit(solution)/shard_map/tkgd,nkd->kgtn/dot_general | solution.py:30
  72.8 66.3 %pmax.7 = f32[256,8]{0,1:T(8,128)S(1)} all-reduce(f32[256,8]{0,1:T(8,128)S(1)} %bitcast.65), channel_id=1, replica_groups=mesh['seq'=32,'head'=4] {'seq'}, use_global_device_ids=true, to_apply=%region_1.0 | all-reduce | flops 2048 | bytes 16384 | tf_op jit(solution)/shard_map/pmax | solution.py:57
  139.1 8.5 %fusion.1 = f32[8,256]{1,0:T(8,128)S(1)} fusion(f32[2048,256,8]{1,0,2:T(8,128)} %get-tuple-element.8, f32[8,256]{1,0:T(8,128)S(1)} %get-tuple-element.7), kind=kLoop, calls=%fused_computation.3 | loop fusion | flops 12580864 | bytes 16793600 | tf_op jit(solution)/shard_map/reduce_sum | solution.py:35
  147.6 7.4 %fusion.4 = f32[128,8,256]{2,0,1:T(8,128)S(1)} fusion(bf16[2048,128,1]{0,1,2:T(8,128)(2,1)S(1)} %reshape.78, f32[2048,256,8]{1,0,2:T(8,128)} %get-tuple-element.8, f32[8,256]{1,0:T(8,128)S(1)} %get-tuple-element.7), kind=kOutput, calls=%fused_computation.6 | convolution fusion | flops 1086324736 | bytes 18358272 | tf_op jit(solution)/shard_map/kgtn,nkd->tkgd/dot_general | solution.py:36
  155.0 0.3 copy.22
  155.4 0.1 copy.21
  155.5 1.3 mul.37
  156.8 1.4 mul.38
  158.2 0.9 multiply_convert_fusion
  159.1 0.0 all-gather.2.cloned.1.call-update
  159.2 0.0 reduce-scatter.2.cloned.1.call-start
  159.2 64.8 %psum.7 = bf16[256,8]{0,1:T(8,128)(2,1)S(1)} all-reduce(bf16[256,8]{0,1:T(8,128)(2,1)S(1)} %get-tuple-element.5), channel_id=1, replica_groups=mesh['seq'=32,'head'=4] {'seq'}, use_global_device_ids=true, to_apply=%region_4.0 | all-reduce | flops 2048 | bytes 8192 | tf_op jit(solution)/shard_map/psum | solution.py:60
  224.0 5.1 %all-gather.2.cloned.1.call-done = bf16[32,256,1024]{2,1,0:T(8,128)(2,1)} async-done(((bf16[1,256,1024]{2,1,0:T(8,128)(2,1)}), bf16[32,256,1024]{2,1,0:T(8,128)(2,1)}) %all-gather.2.cloned.1.call-update) | async-done | bytes 16777232 | tf_op jit(solution)/shard_map/all_gather | solution.py:62
  229.1 9.1 %reduce_sum.23 = bf16[256,1024]{1,0:T(8,128)(2,1)S(1)} reduce(bf16[32,256,1024]{2,1,0:T(8,128)(2,1)} %all-gather.2.cloned.1.call-done, bf16[]{:T(256)} %constant.6.clone.1), dimensions={0}, to_apply=%region_2.0 | reduce | flops 8126464 | bytes 17301506 | tf_op jit(solution)/shard_map/reduce_sum | solution.py:61
  238.2 0.2 copy.26
  238.4 0.1 fusion.6
  238.5 1.0 convolution_convert_fusion.2
  239.5 0.0 reduce-scatter.2.cloned.1.call-update
  239.5 19.9 %reduce-scatter.2.cloned.1.call-done = bf16[64,256]{1,0:T(8,128)(2,1)} async-done(((bf16[256,256]{1,0:T(8,128)(2,1)}), bf16[64,256]{1,0:T(8,128)(2,1)}) %reduce-scatter.2.cloned.1.call-update) | async-done | bytes 32784 | tf_op jit(solution)/shard_map/reduce_scatter | solution.py:66
  (5 shorter events, 0.0 us)
Async XLA Ops:
  6.5 232.0 %copy-start = (bf16[1024,256]{1,0:T(8,128)(2,1)S(1)}, bf16[1024,256]{1,0:T(8,128)(2,1)}, u32[]{:S(2)}) copy-start(bf16[1024,256]{1,0:T(8,128)(2,1)} %param.9) | copy-start | bytes 1572868
  17.1 19.9 %copy-start.1 = (bf16[8,1024]{1,0:T(8,128)(2,1)S(1)}, bf16[8,1024]{1,0:T(8,128)(2,1)}, u32[]{:S(2)}) copy-start(bf16[8,1024]{1,0:T(8,128)(2,1)} %param.8) | copy-start | bytes 49156
  17.1 15.1 %all-to-all-start.1 = ((bf16[512,4,128]{0,2,1:T(8,128)(2,1)}), bf16[512,4,128]{0,2,1:T(8,128)(2,1)S(1)}, u32[]{:S(2)}, u32[]{:S(2)}) async-start(bf16[512,4,128]{0,2,1:T(8,128)(2,1)} %bitcast.2), calls=%async_computation.1 | async-start | bytes 1048576 | tf_op jit(solution)/shard_map/all_to_all | solution.py:52
  32.2 31.8 %all-to-all-start = ((bf16[512,4,128]{0,2,1:T(8,128)(2,1)}), bf16[512,4,128]{0,2,1:T(8,128)(2,1)S(1)}, u32[]{:S(2)}, u32[]{:S(2)}) async-start(bf16[512,4,128]{0,2,1:T(8,128)(2,1)} %bitcast), calls=%async_computation | async-start | bytes 1048576 | tf_op jit(solution)/shard_map/all_to_all | solution.py:53
  37.0 192.1 %all-gather.2.cloned.1.call-start = ((), (), s32[]{:S(2)}) async-start(), calls=%async_computation.3 | async-start | bytes 17301504 | tf_op jit(solution)/shard_map/all_gather | solution.py:62
  159.2 100.3 %reduce-scatter.2.cloned.1.call-start = ((), (), s32[]{:S(2)}) async-start(), calls=%async_computation.4 | async-start | bytes 163840 | tf_op jit(solution)/shard_map/reduce_scatter | solution.py:66
Sparse Core Ops, SparseCore 0:
  159.3 69.7 all-gather.1
  239.6 19.7 reduce-scatter.1
